TPU v7x, 32 devices: a whole 2x2x4 slice. The times are simulated.
32 devices in a mesh: layer: 4 (over y, x), row: 4 (over z), col: 2 (over core).
Axes of the slice: x: 2, y: 2, z: 4, core: 2. Of those that a mesh axis runs over, the one named last changes fastest.
Arguments:
- statistic: float32 [8, 7168, 7168], P('layer', 'row', 'col'), as said below
- eigenbasis: float32 [8, 7168, 1024], P('layer', 'col'), may hold values from -0.0625 to 0.0625
Outputs:
- refreshed: float32 [8, 7168, 1024], P('layer', ('row', 'col'))
Inputs may be any that keep to these rules, and one draw needn't show every extreme that they name: `statistic`: each layer's matrix is symmetric and positive definite.
All inputs are finite; a program needn't handle non-finite values.
Results may differ from a plain program's by a relative error of at most 0.00014.
Values sent between devices are 32-bit elements; how exact they have to be, the bound alone decides.
A program may use at most 192 MiB of HBM per device.

v0:
```python
import jax
import jax.numpy as jnp
from jax import lax
from jax.sharding import PartitionSpec as P


def contract(left_operand, right_operand):
    return lax.dot_general(
        left_operand,
        right_operand,
        (((0,), (0,)), ((), ())),
        precision=lax.Precision.HIGHEST,
        preferred_element_type=jnp.float32,
    )


def multiply(left_operand, right_operand):
    return jnp.dot(
        left_operand,
        right_operand,
        precision=lax.Precision.HIGHEST,
        preferred_element_type=jnp.float32,
    )


def on_device(statistic, eigenbasis):
    results = []
    for member in range(statistic.shape[0]):
        stat_layer = statistic[member]
        basis_layer = eigenbasis[member]
        row_product = lax.psum_scatter(
            multiply(stat_layer, basis_layer), "col", scatter_dimension=0, tiled=True
        )
        gram_matrix = lax.psum(contract(row_product, row_product), ("row", "col"))
        factor = jnp.linalg.cholesky(gram_matrix)
        result = lax.linalg.triangular_solve(
            factor, row_product, left_side=False, lower=True, transpose_a=True
        )
        results.append(result)
    return jnp.stack(results)


def solution(mesh):
    placed = (P("layer", "row", "col"), P("layer", "col", None))
    return jax.shard_map(
        on_device,
        mesh=mesh,
        in_specs=placed,
        out_specs=P("layer", ("row", "col"), None),
        check_vma=False,
    )
```

profile of v0, /device:TPU:0, one launch (start us, length us, event | category | flops | bytes accessed | tf_op | source)
XLA Modules:
  0.0 1133.4 jit_solution(6855643901012336946)
XLA Ops:
  6.5 89.5 %fusion.2 = f32[1792,1024]{1,0:T(8,128)} fusion(f32[2,1792,3584]{2,1,0:T(8,128)} %param.5, f32[2,3584,1024]{2,1,0:T(8,128)} %param.6), kind=kOutput, calls=%fused_computation.6 | convolution fusion | flops 78920024064 | bytes 47710208 | tf_op jit(solution)/shard_map/dot_general | solution.py:18
  96.3 89.6 %fusion = f32[1792,1024]{1,0:T(8,128)} fusion(f32[2,1792,3584]{2,1,0:T(8,128)} %param.5, f32[2,3584,1024]{2,1,0:T(8,128)} %param.6), kind=kOutput, calls=%fused_computation.4 | convolution fusion | flops 78920024064 | bytes 47710208 | tf_op jit(solution)/shard_map/dot_general | solution.py:18
  186.4 17.5 %fusion.150 = f32[1024,1024]{0,1:T(8,128)} fusion(f32[896,1024]{1,0:T(8,128)} %reduce-scatter.3.cloned.1.call-done), kind=kOutput, calls=%fused_computation.321 | convolution fusion | flops 11274289152 | bytes 7864320 | tf_op jit(solution)/shard_map/dot_general | solution.py:8
  204.9 17.5 %fusion.151 = f32[1024,1024]{0,1:T(8,128)} fusion(f32[896,1024]{1,0:T(8,128)} %reduce-scatter.5.cloned.1.call-done), kind=kOutput, calls=%fused_computation.322 | convolution fusion | flops 11274289152 | bytes 7864320 | tf_op jit(solution)/shard_map/dot_general | solution.py:8
  222.4 177.4 %all-reduce.4.cloned.1.call-done = (f32[1024,1024]{0,1:T(8,128)}, f32[1024,1024]{0,1:T(8,128)}) async-done(((f32[1024,1024]{0,1:T(8,128)}, f32[1024,1024]{0,1:T(8,128)}), (f32[1024,1024]{0,1:T(8,128)}, f32[1024,1024]{0,1:T(8,128)})) %all-reduce.4.cloned.1.call-update) | async-done | bytes 8388624 | tf_op jit(solution)/shard_map/psum | solution.py:34
  399.8 5.3 copy.4
  405.2 5.5 copy.6
  410.7 10.4 fusion.10
  423.0 11.7 %cholesky.619 = f32[128,128]{1,0:T(8,128)S(1)} custom-call(f32[128,128]{1,0:T(8,128)S(1)} %cholesky.911), custom_call_target="Cholesky" | custom-call | tf_op jit(solution)/shard_map/jit(cholesky)/cholesky | solution.py:35
  434.8 9.8 custom-call.55
  451.0 11.9 %cholesky.638 = f32[128,128]{1,0:T(8,128)S(1)} custom-call(f32[128,128]{1,0:T(8,128)S(1)} %cholesky.915), custom_call_target="Cholesky" | custom-call | tf_op jit(solution)/shard_map/jit(cholesky)/cholesky | solution.py:35
  464.8 9.8 custom-call.56
  478.0 11.7 %cholesky.659 = f32[128,128]{1,0:T(8,128)S(1)} custom-call(f32[128,128]{1,0:T(8,128)S(1)} %cholesky.920), custom_call_target="Cholesky" | custom-call | tf_op jit(solution)/shard_map/jit(cholesky)/cholesky | solution.py:35
  491.0 9.8 custom-call.57
  504.7 11.7 %cholesky.678 = f32[128,128]{1,0:T(8,128)S(1)} custom-call(f32[128,128]{1,0:T(8,128)S(1)} %cholesky.925), custom_call_target="Cholesky" | custom-call | tf_op jit(solution)/shard_map/jit(cholesky)/cholesky | solution.py:35
  517.7 9.8 custom-call.58
  531.0 11.7 %cholesky.697 = f32[128,128]{1,0:T(8,128)S(1)} custom-call(f32[128,128]{1,0:T(8,128)S(1)} %cholesky.930), custom_call_target="Cholesky" | custom-call | tf_op jit(solution)/shard_map/jit(cholesky)/cholesky | solution.py:35
  543.9 10.0 custom-call.59
  557.2 11.7 %cholesky.716 = f32[128,128]{1,0:T(8,128)S(1)} custom-call(f32[128,128]{1,0:T(8,128)S(1)} %cholesky.935), custom_call_target="Cholesky" | custom-call | tf_op jit(solution)/shard_map/jit(cholesky)/cholesky | solution.py:35
  570.3 9.8 custom-call.60
  583.1 11.9 %cholesky.735 = f32[128,128]{1,0:T(8,128)S(1)} custom-call(f32[128,128]{1,0:T(8,128)S(1)} %cholesky.940), custom_call_target="Cholesky" | custom-call | tf_op jit(solution)/shard_map/jit(cholesky)/cholesky | solution.py:35
  596.3 9.8 custom-call.61
  608.8 11.7 %cholesky.752 = f32[128,128]{1,0:T(8,128)S(1)} custom-call(f32[128,128]{1,0:T(8,128)S(1)} %convolution_subtract_fusion.23), custom_call_target="Cholesky" | custom-call | tf_op jit(solution)/shard_map/jit(cholesky)/cholesky | solution.py:35
  631.5 22.8 %while.4 = (s32[]{:T(128)}, f32[1024,1024]{1,0:T(8,128)}, s32[8,2]{0,1:T(2,128)S(1)}, f32[8,128,128]{2,1,0:T(8,128)S(1)}, s32[]{:T(128)}) while((s32[]{:T(128)}, f32[1024,1024]{1,0:T(8,128)}, s32[8,2]{0,1:T(2,128)S(1)}, f32[8,128,128]{2,1,0:T(8,128)S(1)}, s32[]{:T(128)}) %tuple.114), condition=%wide.while_cond, body=%wide.while_body.sunk | while | flops 2 | bytes 131181 | solution.py:36
  654.3 79.0 %custom-call.62 = f32[8,128,128]{1,2,0:T(8,128)S(1)} custom-call(f32[8,128,128]{2,1,0:T(8,128)S(1)} %get-tuple-element.21), custom_call_target="InvertDiagBlocksLowerTriangular" | custom-call | tf_op jit(solution)/shard_map/triangular_solve/custom-call.7 | solution.py:36
  734.2 11.7 %cholesky.767 = f32[128,128]{1,0:T(8,128)S(1)} custom-call(f32[128,128]{1,0:T(8,128)S(1)} %cholesky.944), custom_call_target="Cholesky" | custom-call | tf_op jit(solution)/shard_map/jit(cholesky)/cholesky | solution.py:35
  745.9 9.8 custom-call.63
  762.2 11.7 %cholesky.786 = f32[128,128]{1,0:T(8,128)S(1)} custom-call(f32[128,128]{1,0:T(8,128)S(1)} %cholesky.948), custom_call_target="Cholesky" | custom-call | tf_op jit(solution)/shard_map/jit(cholesky)/cholesky | solution.py:35
  775.8 9.9 custom-call.64
  789.1 11.7 %cholesky.807 = f32[128,128]{1,0:T(8,128)S(1)} custom-call(f32[128,128]{1,0:T(8,128)S(1)} %cholesky.953), custom_call_target="Cholesky" | custom-call | tf_op jit(solution)/shard_map/jit(cholesky)/cholesky | solution.py:35
  802.1 9.8 custom-call.65
  815.4 11.9 %cholesky.826 = f32[128,128]{1,0:T(8,128)S(1)} custom-call(f32[128,128]{1,0:T(8,128)S(1)} %cholesky.958), custom_call_target="Cholesky" | custom-call | tf_op jit(solution)/shard_map/jit(cholesky)/cholesky | solution.py:35
  828.6 9.8 custom-call.66
  841.9 11.7 %cholesky.845 = f32[128,128]{1,0:T(8,128)S(1)} custom-call(f32[128,128]{1,0:T(8,128)S(1)} %cholesky.963), custom_call_target="Cholesky" | custom-call | tf_op jit(solution)/shard_map/jit(cholesky)/cholesky | solution.py:35
  854.8 9.8 custom-call.67
  868.4 11.7 %cholesky.864 = f32[128,128]{1,0:T(8,128)S(1)} custom-call(f32[128,128]{1,0:T(8,128)S(1)} %cholesky.968), custom_call_target="Cholesky" | custom-call | tf_op jit(solution)/shard_map/jit(cholesky)/cholesky | solution.py:35
  881.5 9.8 custom-call.68
  894.3 11.7 %cholesky.883 = f32[128,128]{1,0:T(8,128)S(1)} custom-call(f32[128,128]{1,0:T(8,128)S(1)} %cholesky.973), custom_call_target="Cholesky" | custom-call | tf_op jit(solution)/shard_map/jit(cholesky)/cholesky | solution.py:35
  907.3 10.0 custom-call.69
  919.9 11.7 %cholesky.900 = f32[128,128]{1,0:T(8,128)S(1)} custom-call(f32[128,128]{1,0:T(8,128)S(1)} %convolution_subtract_fusion.22), custom_call_target="Cholesky" | custom-call | tf_op jit(solution)/shard_map/jit(cholesky)/cholesky | solution.py:35
  942.7 22.8 %while.5 = (s32[]{:T(128)}, f32[1024,1024]{1,0:T(8,128)}, s32[8,2]{0,1:T(2,128)S(1)}, f32[8,128,128]{2,1,0:T(8,128)S(1)}, s32[]{:T(128)}) while((s32[]{:T(128)}, f32[1024,1024]{1,0:T(8,128)}, s32[8,2]{0,1:T(2,128)S(1)}, f32[8,128,128]{2,1,0:T(8,128)S(1)}, s32[]{:T(128)}) %tuple.124), condition=%wide.while_cond.clone, body=%wide.while_body.clone.sunk | while | flops 2 | bytes 131181 | solution.py:36
  965.5 78.8 %custom-call.70 = f32[8,128,128]{1,2,0:T(8,128)S(1)} custom-call(f32[8,128,128]{2,1,0:T(8,128)S(1)} %get-tuple-element.22), custom_call_target="InvertDiagBlocksLowerTriangular" | custom-call | tf_op jit(solution)/shard_map/triangular_solve/custom-call.7 | solution.py:36
  1061.0 5.3 convolution_subtract_fusion.9
  1066.9 5.5 convolution_subtract_fusion.4
  1073.1 6.8 convolution_subtract_fusion.1
  1101.5 5.5 convolution_subtract_fusion.2
  1107.7 6.6 convolution_subtract_fusion
  1118.4 8.0 copy.7
  (170 shorter events, 175.2 us)
Async XLA Ops:
  6.5 179.8 %reduce-scatter.3.cloned.1.call-start = ((), (), s32[]{:S(2)}) async-start(), calls=%async_computation.2 | async-start | bytes 11010048 | tf_op jit(solution)/shard_map/reduce_scatter | solution.py:31
  96.1 108.8 %reduce-scatter.5.cloned.1.call-start = ((), (), s32[]{:S(2)}) async-start(), calls=%async_computation.3 | async-start | bytes 11010048 | tf_op jit(solution)/shard_map/reduce_scatter | solution.py:31
  185.9 213.9 %all-reduce.4.cloned.1.call-start = ((), (), s32[]{:S(2)}) async-start(), calls=%async_computation.4 | async-start | bytes 16777216 | tf_op jit(solution)/shard_map/psum | solution.py:34
  421.1 1.9 copy-start
  1044.4 4.6 copy-start.2
  1072.5 8.1 copy-start.1
Sparse Core Ops, SparseCore 0:
  96.2 18.8 reduce-scatter.2
  186.0 18.8 reduce-scatter.4
  222.5 177.2 all-reduce.3
where the time goes:
time: 1140 us; the launch traced here: 1130 us
  other arithmetic  526 us (46%)
  matrix products  331 us (29%)
  waiting for transfers between devices  178 us (16%)
  local copies, waits for them, and re-layouts  72.2 us (6%)
  between operations  23.9 us (2%)
    another operation x62, other arithmetic, on_device(): factor = jnp.linalg.cholesky(gram_matrix)  345 us
    dot_general x2, matrix products, multiply(): jnp.dot(left_operand, right_operand, precision=lax.Precision.HIGHEST, pre...  179 us
    psum x1, waiting for transfers between devices, on_device(): gram_matrix = lax.psum(contract(row_product, row_product), ('row', 'col'))  177 us
    another operation x5, other arithmetic, on_device(): lax.linalg.triangular_solve(factor, row_product, left_side=False, lower=T...  167 us
    another operation x30, matrix products, on_device(): lax.linalg.triangular_solve(factor, row_product, left_side=False, lower=T...  70.3 us
    another operation x28, matrix products, on_device(): factor = jnp.linalg.cholesky(gram_matrix)  47 us
    another operation x51, local copies, waits for them, and re-layouts, on_device(): lax.linalg.triangular_solve(factor, row_product, left_side=False, lower=T...  45.5 us
    dot_general x2, matrix products, contract(): lax.dot_general(left_operand, right_operand, (((0,), (0,)), ((), ())), pr...  35 us
  transfers between devices with their start and end apart: 3, of which 2 were waited for; matrix products, arithmetic and copies ran while one was open for 9% of the time, Pallas kernels for 0%

commit v1 on v0

--- a/solution.py
+++ b/solution.py
@@ -31,7 +31,12 @@
         row_product = lax.psum_scatter(
             multiply(stat_layer, basis_layer), "col", scatter_dimension=0, tiled=True
         )
-        gram_matrix = lax.psum(contract(row_product, row_product), ("row", "col"))
+
+        def end_knots(a0):
+            part_now = jnp.sum(lax.all_gather(a0, ("row", "col")), 0)
+            return part_now
+
+        gram_matrix = end_knots(contract(row_product, row_product))
         factor = jnp.linalg.cholesky(gram_matrix)
         result = lax.linalg.triangular_solve(
             factor, row_product, left_side=False, lower=True, transpose_a=True

time: 1140 us -> 1270 us (1.11)
  waiting for transfers between devices: 178 us -> 275 us
  other arithmetic: 526 us -> 556 us
    all_gather x0 -> x2, waiting for transfers between devices: none -> 274 us  [end_knots(): part_now = jnp.sum(lax.all_gather(a0, ('row', 'col')), 0)]
    psum x1 -> x0, waiting for transfers between devices: 177 us -> none  [on_device(): gram_matrix = lax.psum(contract(row_product, row_product), ('row', 'col'))]
    reduce_sum x0 -> x2, other arithmetic: none -> 31.8 us  [end_knots(): part_now = jnp.sum(lax.all_gather(a0, ('row', 'col')), 0)]
    another operation x62 -> x60, other arithmetic: 345 us -> 345 us  [on_device(): factor = jnp.linalg.cholesky(gram_matrix)]
  transfers between devices with their start and end apart: 3 -> 4, of which waited for: 2 -> 2; matrix products, arithmetic and copies ran while one was open for 9% -> 36% of each run, Pallas kernels for 0% -> 0%
where the time goes in v1:
time: 1270 us; the launch traced here: 1260 us
  other arithmetic  556 us (44%)
  matrix products  330 us (26%)
  waiting for transfers between devices  275 us (22%)
  local copies, waits for them, and re-layouts  74.2 us (6%)
  between operations  24.5 us (2%)
    another operation x60, other arithmetic, on_device(): factor = jnp.linalg.cholesky(gram_matrix)  345 us
    all_gather x2, waiting for transfers between devices, end_knots(): part_now = jnp.sum(lax.all_gather(a0, ('row', 'col')), 0)  274 us
    dot_general x2, matrix products, multiply(): jnp.dot(left_operand, right_operand, precision=lax.Precision.HIGHEST, pre...  179 us
    another operation x5, other arithmetic, on_device(): lax.linalg.triangular_solve(factor, row_product, left_side=False, lower=T...  167 us
    another operation x30, matrix products, on_device(): lax.linalg.triangular_solve(factor, row_product, left_side=False, lower=T...  70.3 us
    another operation x28, matrix products, on_device(): factor = jnp.linalg.cholesky(gram_matrix)  46.2 us
    another operation x51, local copies, waits for them, and re-layouts, on_device(): lax.linalg.triangular_solve(factor, row_product, left_side=False, lower=T...  45.7 us
    dot_general x2, matrix products, contract(): lax.dot_general(left_operand, right_operand, (((0,), (0,)), ((), ())), pr...  34.7 us
  transfers between devices with their start and end apart: 4, of which 2 were waited for; matrix products, arithmetic and copies ran while one was open for 36% of the time, Pallas kernels for 0%

profile of v1, /device:TPU:0, one launch (start us, length us, event | category | flops | bytes accessed | tf_op | source)
XLA Modules:
  0.0 1261.7 jit_solution(4295637773725847179)
XLA Ops:
  6.5 89.5 %fusion.2 = f32[1792,1024]{1,0:T(8,128)} fusion(f32[2,1792,3584]{2,1,0:T(8,128)} %param.5, f32[2,3584,1024]{2,1,0:T(8,128)} %param.6), kind=kOutput, calls=%fused_computation.6 | convolution fusion | flops 78920024064 | bytes 47710208 | tf_op jit(solution)/shard_map/dot_general | solution.py:18
  96.3 89.6 %fusion = f32[1792,1024]{1,0:T(8,128)} fusion(f32[2,1792,3584]{2,1,0:T(8,128)} %param.5, f32[2,3584,1024]{2,1,0:T(8,128)} %param.6), kind=kOutput, calls=%fused_computation.4 | convolution fusion | flops 78920024064 | bytes 47710208 | tf_op jit(solution)/shard_map/dot_general | solution.py:18
  186.4 17.4 %fusion.150 = f32[1024,1024]{1,0:T(8,128)} fusion(f32[896,1024]{1,0:T(8,128)} %reduce-scatter.3.cloned.1.call-done), kind=kOutput, calls=%fused_computation.321 | convolution fusion | flops 11274289152 | bytes 7864320 | tf_op jit(solution)/shard_map/dot_general | solution.py:8
  204.9 17.3 %fusion.151 = f32[1024,1024]{1,0:T(8,128)} fusion(f32[896,1024]{1,0:T(8,128)} %reduce-scatter.5.cloned.1.call-done), kind=kOutput, calls=%fused_computation.322 | convolution fusion | flops 11274289152 | bytes 7864320 | tf_op jit(solution)/shard_map/dot_general | solution.py:8
  222.3 274.2 %all-gather.5.cloned.1.call-done = f32[8192,1024]{1,0:T(8,128)} async-done(((f32[1024,1024]{1,0:T(8,128)}), f32[8192,1024]{1,0:T(8,128)}) %all-gather.5.cloned.1.call-update) | async-done | bytes 33554448 | tf_op jit(solution)/shard_map/all_gather | solution.py:36
  496.4 17.2 %reduce_sum.18 = f32[1024,1024]{1,0:T(8,128)} reduce(f32[8,1024,1024]{2,1,0:T(8,128)} %bitcast.245, f32[]{:T(128)} %constant.194.clone.1), dimensions={0}, to_apply=%region_1.0 | reduce | flops 7340032 | bytes 37748740 | tf_op jit(solution)/shard_map/reduce_sum | solution.py:36
  513.6 5.7 copy.6
  525.8 11.7 cholesky.619
  537.5 9.8 custom-call.55
  553.7 11.9 cholesky.638
  566.3 9.8 custom-call.56
  579.4 11.7 cholesky.659
  591.8 9.8 custom-call.57
  605.2 12.1 cholesky.678
  617.9 9.8 custom-call.58
  631.2 11.7 cholesky.697
  643.6 10.0 custom-call.59
  656.9 11.7 cholesky.716
  669.2 9.8 custom-call.60
  682.2 11.7 cholesky.735
  694.6 9.8 custom-call.61
  707.0 11.7 cholesky.752
  734.6 22.4 %while.4 = (s32[]{:T(128)}, f32[1024,1024]{1,0:T(8,128)}, s32[8,2]{0,1:T(2,128)S(1)}, f32[8,128,128]{2,1,0:T(8,128)S(1)}, s32[]{:T(128)}) while((s32[]{:T(128)}, f32[1024,1024]{1,0:T(8,128)}, s32[8,2]{0,1:T(2,128)S(1)}, f32[8,128,128]{2,1,0:T(8,128)S(1)}, s32[]{:T(128)}) %tuple.115), condition=%wide.while_cond, body=%wide.while_body.sunk | while | flops 2 | bytes 131181 | solution.py:41
  757.0 78.6 %custom-call.62 = f32[8,128,128]{1,2,0:T(8,128)S(1)} custom-call(f32[8,128,128]{2,1,0:T(8,128)S(1)} %get-tuple-element.21), custom_call_target="InvertDiagBlocksLowerTriangular" | custom-call | tf_op jit(solution)/shard_map/triangular_solve/custom-call.7 | solution.py:41
  835.7 14.7 %reduce_sum.19 = f32[1024,1024]{1,0:T(8,128)} reduce(f32[8,1024,1024]{2,1,0:T(8,128)} %bitcast.244, f32[]{:T(128)} %constant.194.clone.1), dimensions={0}, to_apply=%region_19.22 | reduce | flops 7340032 | bytes 37748740 | tf_op jit(solution)/shard_map/reduce_sum | solution.py:36
  850.4 5.7 copy.7
  862.5 11.7 cholesky.767
  874.2 9.8 custom-call.63
  890.4 11.9 cholesky.786
  902.9 9.8 custom-call.64
  916.1 11.7 cholesky.807
  929.1 9.8 custom-call.65
  942.4 11.9 cholesky.826
  955.6 9.8 custom-call.66
  968.9 11.7 cholesky.845
  981.9 10.2 custom-call.67
  995.4 11.7 cholesky.864
  1008.4 9.8 custom-call.68
  1021.2 11.9 cholesky.883
  1034.3 9.8 custom-call.69
  1046.8 11.7 cholesky.900
  1070.4 23.5 %while.5 = (s32[]{:T(128)}, f32[1024,1024]{1,0:T(8,128)}, s32[8,2]{0,1:T(2,128)S(1)}, f32[8,128,128]{2,1,0:T(8,128)S(1)}, s32[]{:T(128)}) while((s32[]{:T(128)}, f32[1024,1024]{1,0:T(8,128)}, s32[8,2]{0,1:T(2,128)S(1)}, f32[8,128,128]{2,1,0:T(8,128)S(1)}, s32[]{:T(128)}) %tuple.126), condition=%wide.while_cond.clone, body=%wide.while_body.clone.sunk | while | flops 2 | bytes 131181 | solution.py:41
  1093.8 78.8 %custom-call.70 = f32[8,128,128]{1,2,0:T(8,128)S(1)} custom-call(f32[8,128,128]{2,1,0:T(8,128)S(1)} %get-tuple-element.22), custom_call_target="InvertDiagBlocksLowerTriangular" | custom-call | tf_op jit(solution)/shard_map/triangular_solve/custom-call.7 | solution.py:41
  1195.2 5.5 convolution_subtract_fusion.4
  1201.4 6.8 convolution_subtract_fusion.1
  1229.8 5.5 convolution_subtract_fusion.2
  1236.0 6.6 convolution_subtract_fusion
  1246.7 8.0 copy.8
  (176 shorter events, 189.5 us)
Async XLA Ops:
  6.5 179.8 %reduce-scatter.3.cloned.1.call-start = ((), (), s32[]{:S(2)}) async-start(), calls=%async_computation.2 | async-start | bytes 11010048 | tf_op jit(solution)/shard_map/reduce_scatter | solution.py:31
  96.1 108.8 %reduce-scatter.5.cloned.1.call-start = ((), (), s32[]{:S(2)}) async-start(), calls=%async_computation.3 | async-start | bytes 11010048 | tf_op jit(solution)/shard_map/reduce_scatter | solution.py:31
  185.9 310.5 %all-gather.5.cloned.1.call-start = ((), (), s32[]{:S(2)}) async-start(), calls=%async_computation.4 | async-start | bytes 37748736 | tf_op jit(solution)/shard_map/all_gather | solution.py:36
  203.8 631.9 %all-gather.7.cloned.1.call-start = ((), (), s32[]{:S(2)}) async-start(), calls=%async_computation.5 | async-start | bytes 37748736 | tf_op jit(solution)/shard_map/all_gather | solution.py:36
  523.7 2.0 copy-start.1
  860.5 1.9 copy-start
  1172.7 4.6 copy-start.3
  1200.8 8.1 copy-start.2
Sparse Core Ops, SparseCore 0:
  96.2 18.8 reduce-scatter.2
  186.0 18.8 reduce-scatter.4
  206.5 289.8 all-gather.4
  497.9 286.7 all-gather.6
